TPU v7x, 256 devices: a whole 4x4x8 slice. The times are simulated.
256 devices in a mesh: dp: 8 (over z), bin: 32 (over x, y, core).
Axes of the slice: x: 4, y: 4, z: 8, core: 2. Of those that a mesh axis runs over, the one named last changes fastest.
Arguments:
- embeddings: bfloat16 [196608, 256], P(('dp', 'bin')), may hold values from -8 to 8
- bin_ids: int32 [196608], P(('dp', 'bin')), may hold values from 0 to 31, as said below
- spreads: float32 [3], replicated, may hold values from 0.5 to 4
- projection: bfloat16 [256, 256], replicated, may hold values from -0.375 to 0.375
Outputs:
- grad_emb: bfloat16 [196608, 256], P(('dp', 'bin'))
- grad_w: float32 [256, 256], replicated
- loss: float32 [], replicated
Inputs may be any that keep to these rules, and one draw needn't show every extreme that they name: `bin_ids`: among the 768 jets of one device at most 48 share a mass bin, and on every device one bin holds exactly 48 of them.
All inputs are finite; a program needn't handle non-finite values.
Results may differ from a plain program's by a relative error of at most 0.0044.
The roundings to bfloat16 on the way count: a program that leaves them out, or rounds other values in their place, can miss the bound.
Values may be sent and summed in bfloat16 or wider, within the bound.
A program may use at most 64 MiB of HBM per device.

v0:
```python
import jax
import jax.numpy as jnp
from jax import lax
from jax.sharding import PartitionSpec as P


def from_partner(value, axis, bit):
    mask = 2**bit
    pairs = [(source, source ^ mask) for source in range(lax.axis_size(axis))]
    return lax.ppermute(value, axis, pairs)


def tile_terms(xa, mask_a, xb, mask_b, inv_bw):
    rows_a, width = xa.shape
    rows_b = xb.shape[0]
    block = 512
    count = rows_a // block
    sq_b = jnp.sum(jnp.square(xb.astype(jnp.float32)), 1)
    coef = inv_bw / width

    def step(carry, item):
        total, col_sum, back = carry
        xblk, mblk = item
        inner = lax.dot_general(
            xblk, xb, (((1,), (1,)), ((), ())), preferred_element_type=jnp.float32
        )
        sq_a = jnp.sum(jnp.square(xblk.astype(jnp.float32)), 1)
        dist = sq_a[:, None] + sq_b[None, :] - 2.0 * inner
        kern = jnp.zeros(dist.shape, jnp.float32)
        weight = jnp.zeros(dist.shape, jnp.float32)
        for index in range(coef.shape[0]):
            expo = jnp.exp(-dist * coef[index])
            kern = kern + expo
            weight = weight + coef[index] * expo
        pairs = mblk[:, None] * mask_b[None, :]
        total = total + jnp.sum(kern * pairs)
        gram = (weight * pairs).astype(jnp.bfloat16)
        gram_f = gram.astype(jnp.float32)
        part_a = xblk.astype(jnp.float32) * jnp.sum(gram_f, 1)[:, None] - jnp.dot(
            gram, xb, preferred_element_type=jnp.float32
        )
        return ((total, col_sum, back), part_a)

    init = (
        jnp.zeros((), jnp.float32),
        jnp.zeros((rows_b,), jnp.float32),
        jnp.zeros((rows_b, width), jnp.float32),
    )
    (total, col_sum, back), parts = lax.scan(
        step, init, (xa.reshape(count, block, width), mask_a.reshape(count, block))
    )
    part_a = parts.reshape(rows_a, width)
    part_b = xb.astype(jnp.float32) * col_sum[:, None] - back
    return (total, part_a, part_b)


def local(embeddings, bin_ids, spreads, projection):
    rows, width = embeddings.shape
    owners = lax.axis_size("bin")
    slots_per = 2 * rows // owners
    inv_bw = 1.0 / spreads
    feats = jnp.dot(embeddings, projection, preferred_element_type=jnp.float32).astype(jnp.bfloat16)
    onehot = (bin_ids[:, None] == jnp.arange(owners, dtype=jnp.int32)[None, :]).astype(jnp.int32)
    counts = jnp.sum(onehot, 0)
    slot = jnp.sum((jnp.cumsum(onehot, 0) - 1) * onehot, 1)
    outbox = jnp.zeros((owners, slots_per, width), jnp.bfloat16).at[bin_ids, slot].set(feats)
    inbox, arrived = (
        lax.all_to_all(outbox, "bin", split_axis=0, concat_axis=0, tiled=True),
        lax.all_to_all(counts[:, None], "bin", split_axis=0, concat_axis=0, tiled=True),
    )
    mine = inbox.reshape(owners * slots_per, width)
    slot_ids = jnp.arange(slots_per, dtype=jnp.int32)[None, :]
    live = (slot_ids < arrived).astype(jnp.float32).reshape(-1)
    own_n = jnp.maximum(jnp.sum(arrived).astype(jnp.float32), 1.0)
    bit = owners.bit_length() - 2
    partner, partner_arrived = from_partner((mine, arrived), "bin", bit)
    partner_live = (slot_ids < partner_arrived).astype(jnp.float32).reshape(-1)
    partner_n = jnp.maximum(jnp.sum(partner_arrived).astype(jnp.float32), 1.0)
    self_sum, self_part, unused = tile_terms(mine, live, mine, live, inv_bw)
    cross_sum, cross_part, spare = tile_terms(mine, live, partner, partner_live, inv_bw)
    cross_loss = -cross_sum / (own_n * partner_n)
    scale = float(rows * width)
    grad_feat = (
        scale * (-(4.0 / (own_n * own_n)) * self_part + 4.0 / (own_n * partner_n) * cross_part)
    ).astype(jnp.bfloat16)
    local_loss = self_sum / (own_n * own_n) + cross_loss
    homeward = lax.all_to_all(
        grad_feat.reshape(owners, slots_per, width), "bin", split_axis=0, concat_axis=0, tiled=True
    )
    grad_rows = homeward[bin_ids, slot]
    grad_emb = lax.dot_general(
        grad_rows, projection, (((1,), (1,)), ((), ())), preferred_element_type=jnp.float32
    ).astype(jnp.bfloat16)
    partial_w = lax.dot_general(
        embeddings, grad_rows, (((0,), (0,)), ((), ())), preferred_element_type=jnp.float32
    )
    replicas = lax.axis_size("dp")
    tokens_all = float(rows * replicas * owners)
    loss_sum = lax.psum(local_loss, ("dp", "bin"))
    weight_sum = lax.psum(partial_w, ("dp", "bin"))
    return (grad_emb, weight_sum / tokens_all, loss_sum / replicas)


def solution(mesh):
    return jax.shard_map(
        local,
        mesh=mesh,
        in_specs=(P(("dp", "bin"), None), P(("dp", "bin")), P(), P()),
        out_specs=(P(("dp", "bin"), None), P(), P()),
        check_vma=False,
    )
```

profile of v0, /device:TPU:2, one launch (start us, length us, event | category | flops | bytes accessed | tf_op | source)
XLA Modules:
  0.0 560.4 jit_solution(6354406823277336630)
XLA Ops:
  7.9 1.7 reduce-window.6
  11.6 7.6 %all-to-all-start = ((s32[32,1,1]{2,1,0:T(1,128)}), s32[32,1,1]{2,1,0:T(1,128)S(1)}, u32[]{:S(2)}, u32[]{:S(2)}) async-start(s32[32,1,1]{2,1,0:T(1,128)} %copy.13), calls=%async_computation | async-start | bytes 32768 | tf_op jit(solution)/shard_map/all_to_all | solution.py:69
  22.1 83.9 %scatter_fusion = bf16[32,48,256]{2,1,0:T(8,128)(2,1)} fusion(bf16[32,48,256]{2,1,0:T(8,128)(2,1)} %broadcast_in_dim.10, s32[768]{0:T(1024)S(1)} %get-tuple-element.160, bf16[768,256]{1,0:T(8,128)(2,1)S(1)} %convolution_convert_fusion.1), kind=kCustom, calls=%fused_computation.1 | custom fusion | bytes 1185792 | tf_op jit(solution)/shard_map/scatter | solution.py:66
  105.9 8.0 %all-to-all-start.1 = ((bf16[32,48,256]{2,1,0:T(8,128)(2,1)}), bf16[32,48,256]{2,1,0:T(8,128)(2,1)}, u32[]{:S(2)}, u32[]{:S(2)}) async-start(bf16[32,48,256]{2,1,0:T(8,128)(2,1)} %scatter_fusion), calls=%async_computation.1 | async-start | bytes 1572864 | tf_op jit(solution)/shard_map/all_to_all | solution.py:68
  115.3 2.2 collective-permute-start
  118.2 7.4 %collective-permute-done = s32[32,1]{0,1:T(1,128)S(1)} collective-permute-done((s32[32,1]{0,1:T(1,128)S(1)}, s32[32,1]{0,1:T(1,128)S(1)}, u32[]{:S(2)}, u32[]{:S(2)}) %collective-permute-start) | collective-permute-done | bytes 160 | tf_op jit(solution)/shard_map/ppermute | solution.py:10
  127.0 1.7 collective-permute-start.1
  128.6 1.4 multiply_reduce_fusion.1
  130.3 33.9 %while.26 = (s32[]{:T(128)}, f32[]{:T(128)}, f32[3,512,256]{2,1,0:T(8,128)S(1)}, bf16[3,512,256]{2,1,0:T(8,128)(2,1)}, f32[1536]{0:T(1024)S(1)}, /*index=5*/bf16...) while((s32[]{:T(128)}, f32[]{:T(128)}, ...), condition=%wide.region_11.12_spmd.clone, body=%wide.region_7.11_spmd.clone.sunk | while | flops 822609920 | bytes 6076697 | solution.py:49
  132.3 7.0 %convert_reduce_fusion.5 = (f32[512]{0:T(512)S(1)}, bf16[512,1536]{1,0:T(8,128)(2,1)S(1)}, f32[]{:T(128)}) fusion(f32[1536]{0:T(1024)S(1)} %mul.351, f32[512]{0:T(512)S(1)} %bitcast.112, f32[]{:T(128)} %bitcast.97, f32[]{:T(128)} %bitcast.98, f32[]{:T(128)} %bitcast.99, bf16[1536,256]{1,0:T(8,128)(2,1)} %get-tuple-element.400, ...), kind=kOutput, calls=%fused_computation.11.clone.1 | convolution fusion | flops 419167744 | bytes 2641924 | tf_op jit(solution)/shard_map/while/body/eval_jaxpr/dot_general | solution.py:24
  139.2 1.8 fusion.70
  143.6 7.0 %convert_reduce_fusion.5 = (f32[512]{0:T(512)S(1)}, bf16[512,1536]{1,0:T(8,128)(2,1)S(1)}, f32[]{:T(128)}) fusion(f32[1536]{0:T(1024)S(1)} %mul.351, f32[512]{0:T(512)S(1)} %bitcast.112, f32[]{:T(128)} %bitcast.97, f32[]{:T(128)} %bitcast.98, f32[]{:T(128)} %bitcast.99, bf16[1536,256]{1,0:T(8,128)(2,1)} %get-tuple-element.400, ...), kind=kOutput, calls=%fused_computation.11.clone.1 | convolution fusion | flops 419167744 | bytes 2641924 | tf_op jit(solution)/shard_map/while/body/eval_jaxpr/dot_general | solution.py:24
  150.5 1.8 fusion.70
  154.9 7.0 %convert_reduce_fusion.5 = (f32[512]{0:T(512)S(1)}, bf16[512,1536]{1,0:T(8,128)(2,1)S(1)}, f32[]{:T(128)}) fusion(f32[1536]{0:T(1024)S(1)} %mul.351, f32[512]{0:T(512)S(1)} %bitcast.112, f32[]{:T(128)} %bitcast.97, f32[]{:T(128)} %bitcast.98, f32[]{:T(128)} %bitcast.99, bf16[1536,256]{1,0:T(8,128)(2,1)} %get-tuple-element.400, ...), kind=kOutput, calls=%fused_computation.11.clone.1 | convolution fusion | flops 419167744 | bytes 2641924 | tf_op jit(solution)/shard_map/while/body/eval_jaxpr/dot_general | solution.py:24
  161.8 1.8 fusion.70
  165.3 42.6 %while.27 = (s32[]{:T(128)}, f32[]{:T(128)}, f32[3,512,256]{2,1,0:T(8,128)S(1)}, bf16[3,512,256]{2,1,0:T(8,128)(2,1)}, f32[1536]{0:T(1024)}, /*index=5*/bf16[153...) while((s32[]{:T(128)}, f32[]{:T(128)}, ...), condition=%wide.region_18.19_spmd.clone, body=%wide.region_14.18_spmd.clone.sunk | while | flops 822609920 | bytes 9273709 | solution.py:49
  165.3 1.7 fusion.76
  168.2 1.3 fusion.74
  170.4 6.9 %convert_reduce_fusion.6 = (f32[512]{0:T(512)S(1)}, bf16[512,1536]{1,0:T(8,128)(2,1)S(1)}, f32[]{:T(128)}) fusion(f32[1536]{0:T(1024)S(1)} %mul.354, f32[512]{0:T(512)} %bitcast.113, f32[]{:T(128)} %bitcast.108, f32[]{:T(128)} %bitcast.109, f32[]{:T(128)} %bitcast.110, bf16[1536,256]{1,0:T(8,128)(2,1)} %get-tuple-element.370, ...), kind=kOutput, calls=%fused_computation.34.clone.1 | convolution fusion | flops 419167744 | bytes 2643972 | tf_op jit(solution)/shard_map/while/body/eval_jaxpr/dot_general | solution.py:24
  177.3 1.5 fusion.77
  179.5 1.7 fusion.76
  182.4 1.3 fusion.74
  184.6 6.9 %convert_reduce_fusion.6 = (f32[512]{0:T(512)S(1)}, bf16[512,1536]{1,0:T(8,128)(2,1)S(1)}, f32[]{:T(128)}) fusion(f32[1536]{0:T(1024)S(1)} %mul.354, f32[512]{0:T(512)} %bitcast.113, f32[]{:T(128)} %bitcast.108, f32[]{:T(128)} %bitcast.109, f32[]{:T(128)} %bitcast.110, bf16[1536,256]{1,0:T(8,128)(2,1)} %get-tuple-element.370, ...), kind=kOutput, calls=%fused_computation.34.clone.1 | convolution fusion | flops 419167744 | bytes 2643972 | tf_op jit(solution)/shard_map/while/body/eval_jaxpr/dot_general | solution.py:24
  191.5 1.5 fusion.77
  193.7 1.7 fusion.76
  196.6 1.3 fusion.74
  198.8 6.9 %convert_reduce_fusion.6 = (f32[512]{0:T(512)S(1)}, bf16[512,1536]{1,0:T(8,128)(2,1)S(1)}, f32[]{:T(128)}) fusion(f32[1536]{0:T(1024)S(1)} %mul.354, f32[512]{0:T(512)} %bitcast.113, f32[]{:T(128)} %bitcast.108, f32[]{:T(128)} %bitcast.109, f32[]{:T(128)} %bitcast.110, bf16[1536,256]{1,0:T(8,128)(2,1)} %get-tuple-element.370, ...), kind=kOutput, calls=%fused_computation.34.clone.1 | convolution fusion | flops 419167744 | bytes 2643972 | tf_op jit(solution)/shard_map/while/body/eval_jaxpr/dot_general | solution.py:24
  205.7 1.5 fusion.77
  209.1 7.4 %all-to-all-start.2 = ((bf16[32,48,256]{2,1,0:T(8,128)(2,1)}), bf16[32,48,256]{2,1,0:T(8,128)(2,1)S(1)}, u32[]{:S(2)}, u32[]{:S(2)}) async-start(bf16[32,48,256]{2,1,0:T(8,128)(2,1)} %bitcast.111), calls=%async_computation.2 | async-start | bytes 1572864 | tf_op jit(solution)/shard_map/all_to_all | solution.py:87
  216.6 80.5 %psum.15 = f32[]{:T(128)} all-reduce(f32[]{:T(128)S(6)} %add.95), channel_id=1, replica_groups=mesh['dp'=8,'bin'=32] {'dp','bin'}, use_global_device_ids=true, to_apply=%region_20.21 | all-reduce | flops 1 | bytes 8 | tf_op jit(solution)/shard_map/psum | solution.py:99
  297.8 4.4 gather_fusion
  304.4 246.2 %all-reduce.2.cloned.1.call-done = f32[256,256]{0,1:T(8,128)} async-done(((f32[256,256]{0,1:T(8,128)}), f32[256,256]{0,1:T(8,128)}) %all-reduce.2.cloned.1.call-update) | async-done | bytes 262160 | tf_op jit(solution)/shard_map/psum | solution.py:100
  (81 shorter events, 25.7 us)
Async XLA Ops:
  7.2 12.8 %copy-start = (bf16[768,256]{1,0:T(8,128)(2,1)S(1)}, bf16[768,256]{1,0:T(8,128)(2,1)}, u32[]{:S(2)}) copy-start(bf16[768,256]{1,0:T(8,128)(2,1)} %param.8) | copy-start | bytes 1179652
  11.6 94.4 %all-to-all-start = ((s32[32,1,1]{2,1,0:T(1,128)}), s32[32,1,1]{2,1,0:T(1,128)S(1)}, u32[]{:S(2)}, u32[]{:S(2)}) async-start(s32[32,1,1]{2,1,0:T(1,128)} %copy.13), calls=%async_computation | async-start | bytes 32768 | tf_op jit(solution)/shard_map/all_to_all | solution.py:69
  105.9 8.0 %copy-start.7 = (f32[3]{0:T(128)S(1)}, f32[3]{0:T(128)}, u32[]{:S(2)}) copy-start(f32[3]{0:T(128)} %param.10) | copy-start | bytes 40
  105.9 21.0 %all-to-all-start.1 = ((bf16[32,48,256]{2,1,0:T(8,128)(2,1)}), bf16[32,48,256]{2,1,0:T(8,128)(2,1)}, u32[]{:S(2)}, u32[]{:S(2)}) async-start(bf16[32,48,256]{2,1,0:T(8,128)(2,1)} %scatter_fusion), calls=%async_computation.1 | async-start | bytes 1572864 | tf_op jit(solution)/shard_map/all_to_all | solution.py:68
  115.3 10.3 %collective-permute-start = (s32[32,1]{0,1:T(1,128)S(1)}, s32[32,1]{0,1:T(1,128)S(1)}, u32[]{:S(2)}, u32[]{:S(2)}) collective-permute-start(s32[32,1]{0,1:T(1,128)S(1)} %bitcast.115), channel_id=1, source_target_pairs={{0,16},{1,17},{2,18},{3,19},{4,20},{5,21},{6,22},{7,23},{8,24},{9,... | collective-permute-start | bytes 392 | tf_op jit(solution)/shard_map/ppermute | solution.py:10
  125.6 4.7 copy-start.6
  127.0 37.3 %collective-permute-start.1 = (bf16[1536,256]{1,0:T(8,128)(2,1)}, bf16[1536,256]{1,0:T(8,128)(2,1)S(1)}, u32[]{:S(2)}, u32[]{:S(2)}) collective-permute-start(bf16[1536,256]{1,0:T(8,128)(2,1)} %bitcast.4), channel_id=1, source_target_pairs={{0,16},{1,17},{2,18},{3,19},{4,20},{5,21},{6,22},{7,23},{8,24},{9,... | collective-permute-start | bytes 2359304 | tf_op jit(solution)/shard_map/ppermute | solution.py:10
  164.3 0.9 copy-start.1
  165.3 2.9 copy-start.4
  170.4 6.9 %copy-start.2 = (bf16[1536,256]{1,0:T(8,128)(2,1)S(1)}, bf16[1536,256]{1,0:T(8,128)(2,1)}, u32[]{:S(2)}) copy-start(bf16[1536,256]{1,0:T(8,128)(2,1)} %get-tuple-element.370) | copy-start | bytes 2359300 | tf_op jit(solution)/shard_map/while
  177.3 2.2 copy-start.5
  179.5 2.9 copy-start.4
  184.6 7.0 %copy-start.2 = (bf16[1536,256]{1,0:T(8,128)(2,1)S(1)}, bf16[1536,256]{1,0:T(8,128)(2,1)}, u32[]{:S(2)}) copy-start(bf16[1536,256]{1,0:T(8,128)(2,1)} %get-tuple-element.370) | copy-start | bytes 2359300 | tf_op jit(solution)/shard_map/while
  191.5 2.2 copy-start.5
  193.7 2.9 copy-start.4
  198.8 7.0 %copy-start.2 = (bf16[1536,256]{1,0:T(8,128)(2,1)S(1)}, bf16[1536,256]{1,0:T(8,128)(2,1)}, u32[]{:S(2)}) copy-start(bf16[1536,256]{1,0:T(8,128)(2,1)} %get-tuple-element.370) | copy-start | bytes 2359300 | tf_op jit(solution)/shard_map/while
  205.7 2.2 copy-start.5
  209.1 88.7 %all-to-all-start.2 = ((bf16[32,48,256]{2,1,0:T(8,128)(2,1)}), bf16[32,48,256]{2,1,0:T(8,128)(2,1)S(1)}, u32[]{:S(2)}, u32[]{:S(2)}) async-start(bf16[32,48,256]{2,1,0:T(8,128)(2,1)} %bitcast.111), calls=%async_computation.2 | async-start | bytes 1572864 | tf_op jit(solution)/shard_map/all_to_all | solution.py:87
  216.5 334.1 %all-reduce.2.cloned.1.call-start = ((), (), s32[]{:S(2)}) async-start(), calls=%async_computation.3 | async-start | bytes 524288 | tf_op jit(solution)/shard_map/psum | solution.py:100
  297.8 5.5 copy-start.3
Sparse Core Ops, SparseCore 0:
  303.4 247.0 all-reduce.1
where the time goes:
time: 564 us; the launch traced here: 560 us
  waiting for transfers between devices  254 us (45%)
  local copies, waits for them, and re-layouts  99.8 us (18%)
  blocking collectives  80.5 us (14%)
  matrix products  54.8 us (10%)
  starting transfers between devices  26.9 us (5%)
  other arithmetic  23.1 us (4%)
  between operations  17.5 us (3%)
    psum x1, waiting for transfers between devices, local(): weight_sum = lax.psum(partial_w, ('dp', 'bin'))  246 us
    scatter x1, local copies, waits for them, and re-layouts, local(): jnp.zeros((owners, slots_per, width), jnp.bfloat16).at[bin_ids, slot]  83.9 us
    psum x1, blocking collectives, local(): loss_sum = lax.psum(local_loss, ('dp', 'bin'))  80.5 us
    dot_general x6, matrix products, step(): lax.dot_general(xblk, xb, (((1,), (1,)), ((), ())), preferred_element_typ...  41.7 us
  transfers between devices with their start and end apart: 6, of which 2 were waited for; matrix products, arithmetic and copies ran while one was open for 22% of the time, Pallas kernels for 0%

commit v1 on v0

--- a/solution.py
+++ b/solution.py
@@ -97,7 +97,7 @@
     replicas = lax.axis_size("dp")
     tokens_all = float(rows * replicas * owners)
     loss_sum = lax.psum(local_loss, ("dp", "bin"))
-    weight_sum = lax.psum(partial_w, ("dp", "bin"))
+    weight_sum = lax.psum(lax.psum(partial_w, "dp"), "bin")
     return (grad_emb, weight_sum / tokens_all, loss_sum / replicas)
 
 

time: 564 us -> 442 us (0.78)
  waiting for transfers between devices: 254 us -> 113 us
  blocking collectives: 80.5 us -> 98.8 us
  matrix products: 54.8 us -> 64.3 us
  starting transfers between devices: 26.9 us -> 19 us
    psum x1 -> x2, waiting for transfers between devices: 246 us -> 106 us  [local(): weight_sum = lax.psum(lax.psum(partial_w, 'dp'), 'bin')]
    all_to_all x0 -> x1, blocking collectives: none -> 19.2 us  [local(): lax.all_to_all(grad_feat.reshape(owners, slots_per, width), 'bin', split_...]
    all_to_all x1 -> x0, starting transfers between devices: 7.39 us -> none  [local(): lax.all_to_all(grad_feat.reshape(owners, slots_per, width), 'bin', split_...]
    dot_general x6, matrix products: 41.7 us -> 47.6 us  [step(): lax.dot_general(xblk, xb, (((1,), (1,)), ((), ())), preferred_element_typ...]
  transfers between devices with their start and end apart: 6 -> 6, of which waited for: 2 -> 2; matrix products, arithmetic and copies ran while one was open for 22% -> 29% of each run, Pallas kernels for 0% -> 0%
where the time goes in v1:
time: 442 us; the launch traced here: 437 us
  waiting for transfers between devices  113 us (26%)
  local copies, waits for them, and re-layouts  102 us (23%)
  blocking collectives  98.8 us (22%)
  matrix products  64.3 us (15%)
  starting transfers between devices  19 us (4%)
  other arithmetic  18.5 us (4%)
  between operations  17.5 us (4%)
    psum x2, waiting for transfers between devices, local(): weight_sum = lax.psum(lax.psum(partial_w, 'dp'), 'bin')  106 us
    scatter x1, local copies, waits for them, and re-layouts, local(): jnp.zeros((owners, slots_per, width), jnp.bfloat16).at[bin_ids, slot]  84.2 us
    psum x1, blocking collectives, local(): loss_sum = lax.psum(local_loss, ('dp', 'bin'))  79.6 us
    dot_general x6, matrix products, step(): lax.dot_general(xblk, xb, (((1,), (1,)), ((), ())), preferred_element_typ...  47.6 us
    all_to_all x1, blocking collectives, local(): lax.all_to_all(grad_feat.reshape(owners, slots_per, width), 'bin', split_...  19.2 us
    dot_general x6, matrix products, step(): jnp.dot(gram, xb, preferred_element_type=jnp.float32)  13.5 us
  transfers between devices with their start and end apart: 6, of which 2 were waited for; matrix products, arithmetic and copies ran while one was open for 29% of the time, Pallas kernels for 0%

profile of v1, /device:TPU:2, one launch (start us, length us, event | category | flops | bytes accessed | tf_op | source)
XLA Modules:
  0.0 437.4 jit_solution(935200264774674997)
XLA Ops:
  7.9 1.7 reduce-window.6
  11.6 7.6 %all-to-all-start = ((s32[32,1,1]{2,1,0:T(1,128)}), s32[32,1,1]{2,1,0:T(1,128)S(1)}, u32[]{:S(2)}, u32[]{:S(2)}) async-start(s32[32,1,1]{2,1,0:T(1,128)} %copy.13), calls=%async_computation | async-start | bytes 32768 | tf_op jit(solution)/shard_map/all_to_all | solution.py:69
  19.9 1.2 convolution_convert_fusion.1
  22.0 84.2 %scatter_fusion = bf16[32,48,256]{2,1,0:T(8,128)(2,1)} fusion(bf16[32,48,256]{2,1,0:T(8,128)(2,1)} %broadcast_in_dim.10, s32[768]{0:T(1024)S(1)} %get-tuple-element.160, bf16[768,256]{1,0:T(8,128)(2,1)S(1)} %convolution_convert_fusion.1), kind=kCustom, calls=%fused_computation.1 | custom fusion | bytes 1185792 | tf_op jit(solution)/shard_map/scatter | solution.py:66
  106.3 7.4 %all-to-all-start.1 = ((bf16[32,48,256]{2,1,0:T(8,128)(2,1)}), bf16[32,48,256]{2,1,0:T(8,128)(2,1)}, u32[]{:S(2)}, u32[]{:S(2)}) async-start(bf16[32,48,256]{2,1,0:T(8,128)(2,1)} %scatter_fusion), calls=%async_computation.1 | async-start | bytes 1572864 | tf_op jit(solution)/shard_map/all_to_all | solution.py:68
  113.8 1.2 fusion.33
  115.1 2.2 collective-permute-start
  118.0 7.4 %collective-permute-done = s32[32,1]{0,1:T(1,128)S(1)} collective-permute-done((s32[32,1]{0,1:T(1,128)S(1)}, s32[32,1]{0,1:T(1,128)S(1)}, u32[]{:S(2)}, u32[]{:S(2)}) %collective-permute-start) | collective-permute-done | bytes 160 | tf_op jit(solution)/shard_map/ppermute | solution.py:10
  126.7 1.7 collective-permute-start.1
  128.4 1.4 multiply_reduce_fusion.1
  130.1 38.2 %while.26 = (s32[]{:T(128)}, f32[]{:T(128)}, f32[3,512,256]{2,1,0:T(8,128)S(1)}, bf16[3,512,256]{2,1,0:T(8,128)(2,1)}, f32[1536]{0:T(1024)S(1)}, /*index=5*/bf16...) while((s32[]{:T(128)}, f32[]{:T(128)}, ...), condition=%wide.region_11.12_spmd.clone, body=%wide.region_7.11_spmd.clone.sunk | while | flops 822609920 | bytes 6076197 | solution.py:49
  130.9 1.1 fusion.69
  132.0 8.0 %convert_reduce_fusion.5 = (f32[512]{0:T(512)S(1)}, bf16[512,1536]{1,0:T(8,128)(2,1)}, f32[]{:T(128)}) fusion(f32[1536]{0:T(1024)S(1)} %mul.351, f32[512]{0:T(512)S(1)} %bitcast.112, f32[]{:T(128)} %bitcast.97, f32[]{:T(128)} %bitcast.98, f32[]{:T(128)} %bitcast.99, bf16[1536,256]{1,0:T(8,128)(2,1)} %get-tuple-element.400, ...), kind=kOutput, calls=%fused_computation.11.clone.1 | convolution fusion | flops 419167744 | bytes 2641416 | tf_op jit(solution)/shard_map/while/body/eval_jaxpr/dot_general | solution.py:24
  140.6 2.2 fusion.70
  144.7 8.0 %convert_reduce_fusion.5 = (f32[512]{0:T(512)S(1)}, bf16[512,1536]{1,0:T(8,128)(2,1)}, f32[]{:T(128)}) fusion(f32[1536]{0:T(1024)S(1)} %mul.351, f32[512]{0:T(512)S(1)} %bitcast.112, f32[]{:T(128)} %bitcast.97, f32[]{:T(128)} %bitcast.98, f32[]{:T(128)} %bitcast.99, bf16[1536,256]{1,0:T(8,128)(2,1)} %get-tuple-element.400, ...), kind=kOutput, calls=%fused_computation.11.clone.1 | convolution fusion | flops 419167744 | bytes 2641416 | tf_op jit(solution)/shard_map/while/body/eval_jaxpr/dot_general | solution.py:24
  153.3 2.2 fusion.70
  156.4 1.1 fusion.69
  157.5 8.0 %convert_reduce_fusion.5 = (f32[512]{0:T(512)S(1)}, bf16[512,1536]{1,0:T(8,128)(2,1)}, f32[]{:T(128)}) fusion(f32[1536]{0:T(1024)S(1)} %mul.351, f32[512]{0:T(512)S(1)} %bitcast.112, f32[]{:T(128)} %bitcast.97, f32[]{:T(128)} %bitcast.98, f32[]{:T(128)} %bitcast.99, bf16[1536,256]{1,0:T(8,128)(2,1)} %get-tuple-element.400, ...), kind=kOutput, calls=%fused_computation.11.clone.1 | convolution fusion | flops 419167744 | bytes 2641416 | tf_op jit(solution)/shard_map/while/body/eval_jaxpr/dot_general | solution.py:24
  166.0 2.2 fusion.70
  169.3 45.8 %while.27 = (s32[]{:T(128)}, f32[]{:T(128)}, f32[3,512,256]{2,1,0:T(8,128)S(1)}, bf16[3,512,256]{2,1,0:T(8,128)(2,1)}, f32[1536]{0:T(1024)}, /*index=5*/bf16[153...) while((s32[]{:T(128)}, f32[]{:T(128)}, ...), condition=%wide.region_18.19_spmd.clone, body=%wide.region_14.18_spmd.clone.sunk | while | flops 822609920 | bytes 6079325 | solution.py:49
  172.8 1.1 fusion.76
  173.9 7.9 %convert_reduce_fusion.6 = (f32[512]{0:T(512)}, bf16[512,1536]{1,0:T(8,128)(2,1)}, f32[]{:T(128)}) fusion(f32[1536]{0:T(1024)S(1)} %mul.354, f32[512]{0:T(512)S(1)} %bitcast.113, f32[]{:T(128)} %bitcast.108, f32[]{:T(128)} %bitcast.109, f32[]{:T(128)} %bitcast.110, bf16[1536,256]{1,0:T(8,128)(2,1)} %get-tuple-element.370, ...), kind=kOutput, calls=%fused_computation.34.clone.1 | convolution fusion | flops 419167744 | bytes 2643464 | tf_op jit(solution)/shard_map/while/body/eval_jaxpr/dot_general | solution.py:24
  182.3 2.3 fusion.77
  188.0 1.1 fusion.76
  189.1 7.9 %convert_reduce_fusion.6 = (f32[512]{0:T(512)}, bf16[512,1536]{1,0:T(8,128)(2,1)}, f32[]{:T(128)}) fusion(f32[1536]{0:T(1024)S(1)} %mul.354, f32[512]{0:T(512)S(1)} %bitcast.113, f32[]{:T(128)} %bitcast.108, f32[]{:T(128)} %bitcast.109, f32[]{:T(128)} %bitcast.110, bf16[1536,256]{1,0:T(8,128)(2,1)} %get-tuple-element.370, ...), kind=kOutput, calls=%fused_computation.34.clone.1 | convolution fusion | flops 419167744 | bytes 2643464 | tf_op jit(solution)/shard_map/while/body/eval_jaxpr/dot_general | solution.py:24
  197.6 2.3 fusion.77
  204.4 7.9 %convert_reduce_fusion.6 = (f32[512]{0:T(512)}, bf16[512,1536]{1,0:T(8,128)(2,1)}, f32[]{:T(128)}) fusion(f32[1536]{0:T(1024)S(1)} %mul.354, f32[512]{0:T(512)S(1)} %bitcast.113, f32[]{:T(128)} %bitcast.108, f32[]{:T(128)} %bitcast.109, f32[]{:T(128)} %bitcast.110, bf16[1536,256]{1,0:T(8,128)(2,1)} %get-tuple-element.370, ...), kind=kOutput, calls=%fused_computation.34.clone.1 | convolution fusion | flops 419167744 | bytes 2643464 | tf_op jit(solution)/shard_map/while/body/eval_jaxpr/dot_general | solution.py:24
  212.9 2.3 fusion.77
  215.5 19.2 %all_to_all.22 = bf16[32,48,256]{2,1,0:T(8,128)(2,1)S(1)} all-to-all(bf16[32,48,256]{2,1,0:T(8,128)(2,1)S(1)} %bitcast.111), channel_id=1, replica_groups=mesh['dp'=8,'bin'=32] {'bin'}, dimensions={0} | all-to-all | bytes 1572864 | tf_op jit(solution)/shard_map/all_to_all | solution.py:87
  234.7 4.4 %gather_fusion = bf16[768,256]{1,0:T(8,128)(2,1)S(1)} fusion(bf16[32,48,256]{2,1,0:T(8,128)(2,1)S(1)} %all_to_all.22, s32[768]{0:T(1024)S(1)} %get-tuple-element.159), kind=kCustom, calls=%fused_computation | custom fusion | bytes 792576 | tf_op jit(solution)/shard_map/gather | solution.py:90
  240.2 79.6 %psum.23 = f32[]{:T(128)} all-reduce(f32[]{:T(128)S(6)} %add.97), channel_id=1, replica_groups=mesh['dp'=8,'bin'=32] {'dp','bin'}, use_global_device_ids=true, to_apply=%region_21.22 | all-reduce | flops 1 | bytes 8 | tf_op jit(solution)/shard_map/psum | solution.py:99
  321.6 106.0 %all-reduce.5.cloned.1.call-done = f32[256,256]{0,1:T(8,128)} async-done(((f32[256,256]{0,1:T(8,128)}), f32[256,256]{0,1:T(8,128)}) %all-reduce.5.cloned.1.call-update) | async-done | bytes 262160 | tf_op jit(solution)/shard_map/psum | solution.py:100
  (77 shorter events, 25.5 us)
Async XLA Ops:
  7.2 12.8 %copy-start = (bf16[768,256]{1,0:T(8,128)(2,1)S(1)}, bf16[768,256]{1,0:T(8,128)(2,1)}, u32[]{:S(2)}) copy-start(bf16[768,256]{1,0:T(8,128)(2,1)} %param.8) | copy-start | bytes 1179652
  11.6 94.7 %all-to-all-start = ((s32[32,1,1]{2,1,0:T(1,128)}), s32[32,1,1]{2,1,0:T(1,128)S(1)}, u32[]{:S(2)}, u32[]{:S(2)}) async-start(s32[32,1,1]{2,1,0:T(1,128)} %copy.13), calls=%async_computation | async-start | bytes 32768 | tf_op jit(solution)/shard_map/all_to_all | solution.py:69
  106.3 7.5 %copy-start.6 = (f32[3]{0:T(128)S(1)}, f32[3]{0:T(128)}, u32[]{:S(2)}) copy-start(f32[3]{0:T(128)} %param.10) | copy-start | bytes 40
  106.3 20.4 %all-to-all-start.1 = ((bf16[32,48,256]{2,1,0:T(8,128)(2,1)}), bf16[32,48,256]{2,1,0:T(8,128)(2,1)}, u32[]{:S(2)}, u32[]{:S(2)}) async-start(bf16[32,48,256]{2,1,0:T(8,128)(2,1)} %scatter_fusion), calls=%async_computation.1 | async-start | bytes 1572864 | tf_op jit(solution)/shard_map/all_to_all | solution.py:68
  113.7 206.8 %all-reduce.3.cloned.1.call-start = ((), (), s32[]{:S(2)}) async-start(), calls=%async_computation.3 | async-start | bytes 524288 | tf_op jit(solution)/shard_map/psum | solution.py:100
  115.1 10.3 %collective-permute-start = (s32[32,1]{0,1:T(1,128)S(1)}, s32[32,1]{0,1:T(1,128)S(1)}, u32[]{:S(2)}, u32[]{:S(2)}) collective-permute-start(s32[32,1]{0,1:T(1,128)S(1)} %bitcast.115), channel_id=1, source_target_pairs={{0,16},{1,17},{2,18},{3,19},{4,20},{5,21},{6,22},{7,23},{8,24},{9,... | collective-permute-start | bytes 392 | tf_op jit(solution)/shard_map/ppermute | solution.py:10
  126.7 41.6 %collective-permute-start.1 = (bf16[1536,256]{1,0:T(8,128)(2,1)}, bf16[1536,256]{1,0:T(8,128)(2,1)S(1)}, u32[]{:S(2)}, u32[]{:S(2)}) collective-permute-start(bf16[1536,256]{1,0:T(8,128)(2,1)} %bitcast.4), channel_id=1, source_target_pairs={{0,16},{1,17},{2,18},{3,19},{4,20},{5,21},{6,22},{7,23},{8,24},{9,... | collective-permute-start | bytes 2359304 | tf_op jit(solution)/shard_map/ppermute | solution.py:10
  168.3 0.9 copy-start.3
  168.3 0.9 copy-start.1
  169.3 0.6 copy-start.4
  182.3 2.3 copy-start.5
  184.6 0.6 copy-start.4
  197.6 2.3 copy-start.5
  199.9 0.6 copy-start.4
  212.9 2.3 copy-start.5
  239.1 81.5 %copy-start.2 = (bf16[256,256]{1,0:T(8,128)(2,1)S(1)}, bf16[256,256]{1,0:T(8,128)(2,1)}, u32[]{:S(2)}) copy-start(bf16[256,256]{1,0:T(8,128)(2,1)} %param.11) | copy-start | bytes 393220
  240.1 187.5 %all-reduce.5.cloned.1.call-start = ((), (), s32[]{:S(2)}) async-start(), calls=%async_computation.4 | async-start | bytes 524288 | tf_op jit(solution)/shard_map/psum | solution.py:100
Sparse Core Ops, SparseCore 0:
  240.2 73.8 all-reduce.2
  320.7 106.9 all-reduce.4
